TPU v7x, 32 devices: a whole 2x2x4 slice. The times are simulated.
32 devices in a mesh: groups: 2 (over x), expert: 16 (over z, y, core).
Axes of the slice: x: 2, y: 2, z: 4, core: 2. Of those that a mesh axis runs over, the one named last changes fastest.
Arguments:
- routes: int32 [2, 2048, 8], P(None, ('groups', 'expert')), parts along dimension 1, may hold values from 0 to 31, as said below
- gate_weights: float32 [2, 2048, 8], P(None, ('groups', 'expert')), parts along dimension 1, may hold values from 0.05 to 0.5
- grad_out: bfloat16 [2, 2048, 2048], P(None, ('groups', 'expert')), parts along dimension 1, may hold values from -6 to 6
- saved_hidden: bfloat16 [4, 32, 384, 768], P('groups', 'expert'), parts along dimension 0, may hold values from -20 to 20
- down_weight: bfloat16 [32, 768, 2048], P('expert'), may hold values from -0.21875 to 0.21875
Outputs:
- hidden_grad: bfloat16 [2, 2048, 8, 768], P(None, ('groups', 'expert')), parts along dimension 1
- update: bfloat16 [32, 1536, 2048], P('expert', 'groups'), parts along dimension 1
There are 2 independent parts, one for each index of `groups`. A program takes and returns all parts, laid end to end along the dimension named above; an argument that names none is the same for every part. Nothing has to cross between parts.
Inputs may be any that keep to these rules, and one draw needn't show every extreme that they name: `routes`: each token names 8 different experts. In each micro-batch the 64 tokens of one source name any expert at most 24 times, and some expert exactly 24 times by the tokens of every source.
All inputs are finite; a program needn't handle non-finite values.
Results may differ from a plain program's by a relative error of at most 0.011.
Values may be sent and summed in bfloat16 or wider, within the bound.
No kernel may reach another device: no remote copies, remote signals or barrier semaphores. Data moves between devices by JAX's collectives and lax.ppermute only.
A program may use at most 128 MiB of HBM per device.

v0:
```python
import math
import jax
import jax.numpy as jnp
from jax import lax
from jax.sharding import PartitionSpec as P

COEF_A = 3.4445
COEF_B = -4.775
COEF_C = 2.0315


def pick_rows(source_table, row_index):
    return jnp.take(source_table, row_index, axis=0)


def row_places(routes, capacity, experts):
    matches = (routes[..., None] == jnp.arange(experts, dtype=jnp.int32)).astype(jnp.int32)
    per_token = jnp.sum(matches, axis=2)
    earlier = jnp.cumsum(per_token, axis=1) - per_token
    slot_index = jnp.sum(matches * earlier[:, :, None, :], axis=3)
    return routes * capacity + slot_index


def fill_slots(places, gate_weights, grad_out, slot_total):
    batches, tokens, top_count = places.shape
    flat_place = places.reshape(batches, 1, tokens * top_count)
    target = jnp.arange(slot_total, dtype=jnp.int32)[None, :, None]
    matched = flat_place == target
    token_ids = (jnp.arange(tokens * top_count, dtype=jnp.int32) // top_count)[None, None, :]
    source_token = jnp.sum(jnp.where(matched, token_ids, 0), axis=2)
    slot_gate = jnp.sum(
        jnp.where(matched, gate_weights.reshape(batches, 1, tokens * top_count), 0.0), axis=2
    )
    picked_rows = jax.vmap(pick_rows)(grad_out, source_token)
    return (slot_gate[:, :, None] * picked_rows.astype(jnp.float32)).astype(jnp.bfloat16)


def orthogonal_step(weight_grad, model_width):
    hidden_width = weight_grad.shape[1]
    gram_raw = jnp.einsum(
        "efd,egd->efg", weight_grad, weight_grad, preferred_element_type=jnp.float32
    )
    frob_norm = jnp.sqrt(jnp.sum(gram_raw * gram_raw, axis=(1, 2))) + 1e-06
    gram_unit = gram_raw / frob_norm[:, None, None]
    gram_half = gram_unit.astype(jnp.bfloat16)
    identity = jnp.eye(hidden_width, dtype=jnp.float32)[None]
    square_first = jnp.einsum(
        "efg,egh->efh", gram_half, gram_half, preferred_element_type=jnp.float32
    )
    poly_first = (COEF_A * identity + COEF_B * gram_unit + COEF_C * square_first).astype(
        jnp.bfloat16
    )
    left_product = jnp.einsum(
        "efg,egh->efh", poly_first, gram_half, preferred_element_type=jnp.float32
    ).astype(jnp.bfloat16)
    gram_next = jnp.einsum(
        "efg,egh->efh", left_product, poly_first, preferred_element_type=jnp.float32
    )
    next_half = gram_next.astype(jnp.bfloat16)
    square_next = jnp.einsum(
        "efg,egh->efh", next_half, next_half, preferred_element_type=jnp.float32
    )
    poly_next = (COEF_A * identity + COEF_B * gram_next + COEF_C * square_next).astype(jnp.bfloat16)
    product = jnp.einsum("efg,egh->efh", poly_next, poly_first, preferred_element_type=jnp.float32)
    scaling = math.sqrt(model_width) / jnp.sqrt(frob_norm)
    combined = (product * scaling[:, None, None]).astype(jnp.bfloat16)
    return jnp.einsum(
        "efg,egd->efd", combined, weight_grad, preferred_element_type=jnp.float32
    ).astype(jnp.bfloat16)


def local(routes, gate_weights, grad_out, saved_hidden, down_weight):
    devices = lax.axis_size("expert")
    local_experts = down_weight.shape[0]
    hidden_width = down_weight.shape[1]
    model_width = down_weight.shape[2]
    experts = devices * local_experts
    batches = saved_hidden.shape[0]
    slot_count = saved_hidden.shape[2]
    capacity = slot_count // devices
    tokens = routes.shape[1]
    top_count = routes.shape[2]
    places = row_places(routes, capacity, experts)
    outgoing = fill_slots(places, gate_weights, grad_out, experts * capacity)
    outgoing = outgoing.reshape(batches, devices, local_experts, capacity, model_width)
    arrived = lax.all_to_all(outgoing, "expert", split_axis=1, concat_axis=3, tiled=True)
    received = arrived.reshape(batches, local_experts, slot_count, model_width)
    slot_grad = jnp.einsum(
        "mjsd,jfd->mjsf", received, down_weight, preferred_element_type=jnp.float32
    ).astype(jnp.bfloat16)
    returned = lax.all_to_all(
        slot_grad.reshape(batches, 1, local_experts, slot_count, hidden_width),
        "expert",
        split_axis=3,
        concat_axis=1,
        tiled=True,
    )
    back_table = returned.reshape(batches, experts * capacity, hidden_width)
    hidden_grad = jax.vmap(pick_rows)(back_table, places.reshape(batches, tokens * top_count))
    hidden_grad = hidden_grad.reshape(batches, tokens, top_count, hidden_width)
    weight_grad = jnp.einsum(
        "mjsf,mjsd->jfd", saved_hidden, received, preferred_element_type=jnp.float32
    ).astype(jnp.bfloat16)
    update = orthogonal_step(weight_grad, model_width)
    return (hidden_grad, update)


def solution(mesh):
    in_specs = (
        P(None, ("groups", "expert"), None),
        P(None, ("groups", "expert"), None),
        P(None, ("groups", "expert"), None),
        P("groups", "expert", None, None),
        P("expert", None, None),
    )
    out_specs = (P(None, ("groups", "expert"), None, None), P("expert", "groups", None))
    return jax.shard_map(local, mesh=mesh, in_specs=in_specs, out_specs=out_specs, check_vma=False)
```

profile of v0, /device:TPU:15, one launch (start us, length us, event | category | flops | bytes accessed | tf_op | source)
XLA Modules:
  0.0 294.3 jit_solution(15632452333136307427)
XLA Ops:
  0.6 0.0 copy-start
  0.6 0.0 copy-start.2
  0.7 0.9 convert_reduce_fusion
  1.6 0.1 copy.40
  1.7 0.1 reduce_window_sum.11
  1.8 0.1 copy.42
  1.8 0.8 select_reduce_fusion.2
  2.6 0.7 compare_and_fusion.1
  3.3 0.1 copy.44
  3.4 0.1 reshape.126
  3.5 0.4 select_reduce_fusion
  4.0 0.1 reduce_sum.53
  4.2 0.8 copy.45
  5.0 0.1 broadcast_in_dim.56
  5.1 0.4 select_reduce_fusion.1
  5.5 0.1 mul.60
  5.7 0.0 copy-done.2
  5.7 33.1 %gather_fusion = bf16[1536,2048]{1,0:T(8,128)(2,1)} fusion(bf16[2,64,2048]{2,1,0:T(8,128)(2,1)S(1)} %copy-done.2, s32[1536]{0:T(1024)S(1)} %reshape.131), kind=kCustom, calls=%fused_computation | custom fusion | bytes 12595200 | tf_op jit(solution)/shard_map/vmap(jit(_take))/gather | solution.py:13
  38.8 7.2 %multiply_convert_fusion = bf16[2,16,2,24,2048]{4,3,0,2,1:T(8,128)(2,1)} fusion(bf16[2,16,2,24,2048]{4,3,2,1,0:T(8,128)(2,1)} %bitcast.42, f32[2,16,2,24]{3,0,2,1:T(2,128)S(1)} %copy.46, pred[2,16,2,24]{3,0,2,1:T(4,128)(4,1)S(1)} %copy.47), kind=kLoop, calls=%fused_computation.3 | loop fusion | flops 12582912 | bytes 12590592 | tf_op jit(solution)/shard_map/convert_element_type | solution.py:35
  45.9 6.5 %all-to-all-start = ((bf16[2,16,2,24,2048]{4,3,0,2,1:T(8,128)(2,1)}), bf16[2,16,2,24,2048]{4,3,0,2,1:T(8,128)(2,1)}, u32[]{:S(2)}, u32[]{:S(2)}) async-start(bf16[2,16,2,24,2048]{4,3,0,2,1:T(8,128)(2,1)} %multiply_convert_fusion), calls=%async_computation | async-start | bytes 12582912 | tf_op jit(solution)/shard_map/all_to_all | solution.py:86
  52.5 0.1 reshape.130
  52.6 0.1 copy.43
  52.7 1.5 fusion.12
  54.3 135.6 %all-to-all-done = bf16[2,16,2,24,2048]{4,3,0,2,1:T(8,128)(2,1)} async-done(((bf16[2,16,2,24,2048]{4,3,0,2,1:T(8,128)(2,1)}), bf16[2,16,2,24,2048]{4,3,0,2,1:T(8,128)(2,1)}, u32[]{:S(2)}, u32[]{:S(2)}) %all-to-all-start) | async-done | bytes 6291488 | tf_op jit(solution)/shard_map/all_to_all | solution.py:86
  189.9 3.4 %copy.49 = bf16[2,1,2,16,24,2048]{5,4,3,0,2,1:T(8,128)(2,1)S(1)} copy(bf16[2,1,2,16,24,2048]{5,4,0,2,3,1:T(8,128)(2,1)} %bitcast.3) | data formatting | bytes 12582912 | tf_op jit(solution)/shard_map/all_to_all | solution.py:86
  193.2 8.1 %convert_bitcast_fusion = bf16[2,1,2,384,768]{4,3,0,2,1:T(8,128)(2,1)S(1)} fusion(bf16[2,2,384,2048]{3,2,0,1:T(8,128)(2,1)S(1)} %bitcast.44, bf16[2,768,2048]{2,1,0:T(8,128)(2,1)} %param.9), kind=kOutput, calls=%fused_computation.27 | convolution fusion | flops 4833017856 | bytes 14942208 | tf_op jit(solution)/shard_map/mjsd,jfd->mjsf/dot_general | solution.py:88
  201.4 0.0 copy-done
  201.4 7.3 %bitcast_convert_fusion = bf16[2,2048,768]{2,1,0:T(8,128)(2,1)} fusion(bf16[2,2,384,2048]{3,2,0,1:T(8,128)(2,1)S(1)} %bitcast.45, bf16[2,2,384,768]{3,2,1,0:T(8,128)(2,1)S(1)} %copy-done), kind=kOutput, calls=%fused_computation.2 | convolution fusion | flops 4834983936 | bytes 14942208 | tf_op jit(solution)/shard_map/mjsf,mjsd->jfd/dot_general | solution.py:101
  208.7 3.8 %copy.50 = bf16[2,1,2,384,768]{4,0,2,1,3:T(2,128)(2,1)} copy(bf16[2,1,2,384,768]{4,3,0,2,1:T(8,128)(2,1)S(1)} %convert_bitcast_fusion) | data formatting | bytes 4718592 | tf_op jit(solution)/shard_map/reshape | solution.py:92
  212.5 4.8 %all-to-all-start.1 = ((bf16[2,1,2,384,768]{4,0,2,1,3:T(2,128)(2,1)}), bf16[2,1,2,384,768]{4,0,2,1,3:T(2,128)(2,1)S(1)}, u32[]{:S(2)}, u32[]{:S(2)}) async-start(bf16[2,1,2,384,768]{4,0,2,1,3:T(2,128)(2,1)} %copy.50), calls=%async_computation.1 | async-start | bytes 4718592 | tf_op jit(solution)/shard_map/all_to_all | solution.py:91
  217.3 0.0 copy-start.3
  217.3 9.5 %multiply_reduce_fusion = (f32[2]{0:T(128)S(1)}, f32[2,768,768]{2,1,0:T(8,128)S(1)}) fusion(bf16[2,2048,768]{2,1,0:T(8,128)(2,1)} %bitcast_convert_fusion), kind=kOutput, calls=%fused_computation.10 | convolution fusion | flops 4834197504 | bytes 11010056 | tf_op jit(solution)/shard_map/efd,egd->efg/dot_general | solution.py:40
  226.7 0.0 copy-start.4
  226.8 2.2 copy-done.4
  228.9 0.0 copy-done.3
  228.9 3.8 %add_convert_fusion.1 = bf16[2,768,768]{2,1,0:T(8,128)(2,1)} fusion(f32[768,768]{1,0:T(8,128)S(1)} %copy-done.3, f32[2,768,768]{2,1,0:T(8,128)S(1)} %get-tuple-element.7, f32[2]{0:T(128)S(1)} %get-tuple-element.5), kind=kOutput, calls=%fused_computation.9 | convolution fusion | flops 1821376512 | bytes 9437192 | tf_op jit(solution)/shard_map/efg,egh->efh/dot_general | solution.py:47
  232.7 9.9 %fusion.7 = f32[2,768,768]{2,1,0:T(8,128)} fusion(bf16[2,768,768]{2,1,0:T(8,128)(2,1)} %add_convert_fusion.1, f32[2,768,768]{2,1,0:T(8,128)} %copy-done.4, f32[2]{0:T(128)S(1)} %get-tuple-element.5), kind=kOutput, calls=%fused_computation.20 | convolution fusion | flops 3627417600 | bytes 11796488 | tf_op jit(solution)/shard_map/efg,egh->efh/dot_general | solution.py:56
  242.6 13.0 %fusion.2 = f32[2,768,768]{2,1,0:T(8,128)} fusion(bf16[2,768,768]{2,1,0:T(8,128)(2,1)} %add_convert_fusion.1, f32[2,768,768]{2,1,0:T(8,128)} %fusion.7, f32[768,768]{1,0:T(8,128)} %fusion.12), kind=kOutput, calls=%fused_computation.15 | convolution fusion | flops 3630956544 | bytes 14155776 | tf_op jit(solution)/shard_map/efg,egh->efh/dot_general | solution.py:64
  255.6 10.3 %convolution_convert_fusion = bf16[2,768,2048]{2,1,0:T(8,128)(2,1)} fusion(bf16[2,2048,768]{2,1,0:T(8,128)(2,1)} %bitcast_convert_fusion, f32[2,768,768]{2,1,0:T(8,128)} %fusion.2, f32[2]{0:T(128)S(1)} %get-tuple-element.4), kind=kOutput, calls=%fused_computation.11 | convolution fusion | flops 4837343232 | bytes 17301512 | tf_op jit(solution)/shard_map/efg,egd->efd/dot_general | solution.py:67
  265.9 4.4 %all-to-all-done.1 = bf16[2,1,2,384,768]{4,0,2,1,3:T(2,128)(2,1)S(1)} async-done(((bf16[2,1,2,384,768]{4,0,2,1,3:T(2,128)(2,1)}), bf16[2,1,2,384,768]{4,0,2,1,3:T(2,128)(2,1)S(1)}, u32[]{:S(2)}, u32[]{:S(2)}) %all-to-all-start.1) | async-done | bytes 2359328 | tf_op jit(solution)/shard_map/all_to_all | solution.py:91
  270.3 1.7 copy.51
  272.0 0.0 copy-start.1
  272.0 19.4 %gather_fusion.1 = bf16[1024,768]{1,0:T(8,128)(2,1)} fusion(bf16[2,768,768]{2,1,0:T(8,128)(2,1)} %bitcast.40, s32[1024]{0:T(1024)S(1)} %bitcast.41), kind=kCustom, calls=%fused_computation.1 | custom fusion | bytes 3153920 | tf_op jit(solution)/shard_map/vmap(jit(_take))/gather | solution.py:13
  291.5 2.8 broadcast_select_fusion
  294.2 0.0 copy-done.1
  (10 shorter events, 0.2 us)
Async XLA Ops:
  0.6 200.7 %copy-start = (bf16[2,2,384,768]{3,2,1,0:T(8,128)(2,1)S(1)}, bf16[2,2,384,768]{3,2,1,0:T(8,128)(2,1)}, u32[]{:S(2)}) copy-start(bf16[2,2,384,768]{3,2,1,0:T(8,128)(2,1)} %param.8) | copy-start | bytes 7077892
  0.6 5.0 %copy-start.2 = (bf16[2,64,2048]{2,1,0:T(8,128)(2,1)S(1)}, bf16[2,64,2048]{2,1,0:T(8,128)(2,1)}, u32[]{:S(2)}) copy-start(bf16[2,64,2048]{2,1,0:T(8,128)(2,1)} %param.7) | copy-start | bytes 1572868
  45.9 143.9 %all-to-all-start = ((bf16[2,16,2,24,2048]{4,3,0,2,1:T(8,128)(2,1)}), bf16[2,16,2,24,2048]{4,3,0,2,1:T(8,128)(2,1)}, u32[]{:S(2)}, u32[]{:S(2)}) async-start(bf16[2,16,2,24,2048]{4,3,0,2,1:T(8,128)(2,1)} %multiply_convert_fusion), calls=%async_computation | async-start | bytes 12582912 | tf_op jit(solution)/shard_map/all_to_all | solution.py:86
  212.5 57.8 %all-to-all-start.1 = ((bf16[2,1,2,384,768]{4,0,2,1,3:T(2,128)(2,1)}), bf16[2,1,2,384,768]{4,0,2,1,3:T(2,128)(2,1)S(1)}, u32[]{:S(2)}, u32[]{:S(2)}) async-start(bf16[2,1,2,384,768]{4,0,2,1,3:T(2,128)(2,1)} %copy.50), calls=%async_computation.1 | async-start | bytes 4718592 | tf_op jit(solution)/shard_map/all_to_all | solution.py:91
  217.3 11.7 %copy-start.3 = (f32[768,768]{1,0:T(8,128)S(1)}, f32[768,768]{1,0:T(8,128)}, u32[]{:S(2)}) copy-start(f32[768,768]{1,0:T(8,128)} %fusion.12) | copy-start | bytes 7077892
  226.7 2.2 copy-start.4
  272.0 22.2 %copy-start.1 = (bf16[2,2,384,768]{3,2,1,0:T(8,128)(2,1)S(1)}, bf16[2,2,384,768]{3,2,1,0:T(8,128)(2,1)}, u32[]{:S(2)}) copy-start(bf16[2,2,384,768]{3,2,1,0:T(8,128)(2,1)} %param.8) | copy-start | bytes 7077892
where the time goes:
time: 295 us; the launch traced here: 294 us
  waiting for transfers between devices  140 us (47%)
  local copies, waits for them, and re-layouts  65.4 us (22%)
  matrix products  61.9 us (21%)
  other arithmetic  14.9 us (5%)
  starting transfers between devices  11.3 us (4%)
    all_to_all x1, waiting for transfers between devices, local(): lax.all_to_all(outgoing, 'expert', split_axis=1, concat_axis=3, tiled=True)  136 us
    gather x3, local copies, waits for them, and re-layouts, pick_rows(): return jnp.take(source_table, row_index, axis=0)  52.6 us
    dot_general x1, matrix products, orthogonal_step(): jnp.einsum('efg,egh->efh', poly_next, poly_first, preferred_element_type=...  13 us
    dot_general x1, matrix products, orthogonal_step(): jnp.einsum('efg,egd->efd', combined, weight_grad, preferred_element_type=...  10.3 us
    dot_general x1, matrix products, orthogonal_step(): jnp.einsum('efg,egh->efh', left_product, poly_first, preferred_element_ty...  9.89 us
    dot_general x1, matrix products, orthogonal_step(): jnp.einsum('efd,egd->efg', weight_grad, weight_grad, preferred_element_ty...  9.48 us
    dot_general x1, matrix products, local(): jnp.einsum('mjsd,jfd->mjsf', received, down_weight, preferred_element_typ...  8.13 us
    dot_general x1, matrix products, local(): jnp.einsum('mjsf,mjsd->jfd', saved_hidden, received, preferred_element_ty...  7.3 us
  transfers between devices with their start and end apart: 2, of which 2 were waited for; matrix products, arithmetic and copies ran while one was open for 16% of the time, Pallas kernels for 0%

commit v1 on v0

--- a/solution.py
+++ b/solution.py
@@ -7,6 +7,15 @@
 COEF_A = 3.4445
 COEF_B = -4.775
 COEF_C = 2.0315
+
+
+def state_the_loops(sample, row_axis):
+    return jnp.concatenate(
+        jax.lax.all_to_all(
+            jnp.stack(jnp.split(sample, jax.lax.axis_size(row_axis), 1), 0), row_axis, 0, 0
+        ),
+        3,
+    )
 
 
 def pick_rows(source_table, row_index):
@@ -83,7 +92,7 @@
     places = row_places(routes, capacity, experts)
     outgoing = fill_slots(places, gate_weights, grad_out, experts * capacity)
     outgoing = outgoing.reshape(batches, devices, local_experts, capacity, model_width)
-    arrived = lax.all_to_all(outgoing, "expert", split_axis=1, concat_axis=3, tiled=True)
+    arrived = state_the_loops(outgoing, "expert")
     received = arrived.reshape(batches, local_experts, slot_count, model_width)
     slot_grad = jnp.einsum(
         "mjsd,jfd->mjsf", received, down_weight, preferred_element_type=jnp.float32

time: 295 us -> 305 us (1.034)
  local copies, waits for them, and re-layouts: 65.4 us -> 77.7 us
    unnamed x12 -> x27, local copies, waits for them, and re-layouts: 2.99 us -> 14.6 us
    all_to_all x1 -> x0, local copies, waits for them, and re-layouts: 3.36 us -> none  [local(): lax.all_to_all(outgoing, 'expert', split_axis=1, concat_axis=3, tiled=True)]
    reshape x0 -> x1, local copies, waits for them, and re-layouts: none -> 3.36 us  [state_the_loops(): jnp.concatenate(jax.lax.all_to_all(jnp.stack(jnp.split(sample, jax.lax.ax...]
where the time goes in v1:
time: 305 us; the launch traced here: 304 us
  waiting for transfers between devices  140 us (46%)
  local copies, waits for them, and re-layouts  77.7 us (25%)
  matrix products  61.9 us (20%)
  other arithmetic  12.1 us (4%)
  starting transfers between devices  11.3 us (4%)
    all_to_all x1, waiting for transfers between devices, state_the_loops(): jax.lax.all_to_all(jnp.stack(jnp.split(sample, jax.lax.axis_size(row_axis...  136 us
    gather x3, local copies, waits for them, and re-layouts, pick_rows(): return jnp.take(source_table, row_index, axis=0)  52.6 us
    unnamed x27, local copies, waits for them, and re-layouts  14.6 us
    dot_general x1, matrix products, orthogonal_step(): jnp.einsum('efg,egh->efh', poly_next, poly_first, preferred_element_type=...  13 us
    dot_general x1, matrix products, orthogonal_step(): jnp.einsum('efg,egd->efd', combined, weight_grad, preferred_element_type=...  10.3 us
    dot_general x1, matrix products, orthogonal_step(): jnp.einsum('efg,egh->efh', left_product, poly_first, preferred_element_ty...  9.89 us
    dot_general x1, matrix products, orthogonal_step(): jnp.einsum('efd,egd->efg', weight_grad, weight_grad, preferred_element_ty...  9.48 us
    dot_general x1, matrix products, local(): jnp.einsum('mjsd,jfd->mjsf', received, down_weight, preferred_element_typ...  8.13 us
  transfers between devices with their start and end apart: 2, of which 2 were waited for; matrix products, arithmetic and copies ran while one was open for 16% of the time, Pallas kernels for 0%

profile of v1, /device:TPU:15, one launch (start us, length us, event | category | flops | bytes accessed | tf_op | source)
XLA Modules:
  0.0 303.8 jit_solution(15014651220521665072)
XLA Ops:
  0.6 0.0 copy-start
  0.6 0.0 copy-start.2
  0.7 0.9 convert_reduce_fusion
  1.6 0.1 copy.70
  1.7 0.1 reduce_window_sum.11
  1.8 0.1 copy.72
  1.8 0.8 select_reduce_fusion.2
  2.6 0.7 compare_and_fusion.1
  3.3 0.1 copy.74
  3.4 0.1 reshape.125
  3.5 0.4 select_reduce_fusion
  4.0 0.1 reduce_sum.53
  4.2 0.8 copy.75
  5.0 0.1 broadcast_in_dim.56
  5.1 0.4 select_reduce_fusion.1
  5.5 0.1 mul.60
  5.7 0.0 copy-done.2
  5.7 33.1 %gather_fusion = bf16[1536,2048]{1,0:T(8,128)(2,1)} fusion(bf16[2,64,2048]{2,1,0:T(8,128)(2,1)S(1)} %copy-done.2, s32[1536]{0:T(1024)S(1)} %reshape.130), kind=kCustom, calls=%fused_computation | custom fusion | bytes 12595200 | tf_op jit(solution)/shard_map/vmap(jit(_take))/gather | solution.py:22
  38.8 4.4 %multiply_convert_fusion = bf16[2,16,2,24,2048]{4,3,0,2,1:T(8,128)(2,1)S(1)} fusion(bf16[2,16,2,24,2048]{4,3,2,1,0:T(8,128)(2,1)} %bitcast.104, f32[2,16,2,24]{3,0,2,1:T(2,128)S(1)} %copy.76, pred[2,16,2,24]{3,0,2,1:T(4,128)(4,1)S(1)} %copy.77), kind=kLoop, calls=%fused_computation.3 | loop fusion | flops 12582912 | bytes 12590592 | tf_op jit(solution)/shard_map/convert_element_type | solution.py:44
  43.1 0.8 fusion.41
  43.9 0.8 fusion.40
  44.7 0.8 fusion.39
  45.5 0.8 fusion.38
  46.2 0.8 fusion.37
  47.0 0.8 fusion.36
  47.8 0.8 fusion.35
  48.6 0.8 fusion.34
  49.3 0.8 fusion.33
  50.1 0.8 fusion.32
  50.9 0.8 fusion.31
  51.7 0.8 fusion.30
  52.4 0.8 fusion.29
  53.2 0.8 fusion.28
  54.0 0.8 fusion.27
  54.7 0.8 fusion.26
  55.5 6.5 %all-to-all-start = ((bf16[16,2,1,2,24,2048]{5,4,1,3,2,0:T(8,128)(2,1)}), bf16[16,2,1,2,24,2048]{5,4,1,3,2,0:T(8,128)(2,1)}, u32[]{:S(2)}, u32[]{:S(2)}) async-start(bf16[16,2,1,2,24,2048]{5,4,1,3,2,0:T(8,128)(2,1)} %fusion.26), calls=%async_computation | async-start | bytes 12582912 | tf_op jit(solution)/shard_map/all_to_all | solution.py:14
  62.0 0.1 reshape.129
  62.1 0.1 copy.73
  62.3 1.5 fusion.12
  63.8 135.6 %all-to-all-done = bf16[16,2,1,2,24,2048]{5,4,1,3,2,0:T(8,128)(2,1)} async-done(((bf16[16,2,1,2,24,2048]{5,4,1,3,2,0:T(8,128)(2,1)}), bf16[16,2,1,2,24,2048]{5,4,1,3,2,0:T(8,128)(2,1)}, u32[]{:S(2)}, u32[]{:S(2)}) %all-to-all-start) | async-done | bytes 6291488 | tf_op jit(solution)/shard_map/all_to_all | solution.py:14
  199.4 3.4 %copy.79 = bf16[2,1,2,16,24,2048]{5,4,3,0,2,1:T(8,128)(2,1)S(1)} copy(bf16[2,1,2,16,24,2048]{5,4,0,2,1,3:T(8,128)(2,1)} %bitcast.18) | data formatting | bytes 12582912 | tf_op jit(solution)/shard_map/reshape | solution.py:13
  202.8 8.1 %convert_bitcast_fusion = bf16[2,1,2,384,768]{4,3,0,2,1:T(8,128)(2,1)S(1)} fusion(bf16[2,2,384,2048]{3,2,0,1:T(8,128)(2,1)S(1)} %bitcast.106, bf16[2,768,2048]{2,1,0:T(8,128)(2,1)} %param.9), kind=kOutput, calls=%fused_computation.27 | convolution fusion | flops 4833017856 | bytes 14942208 | tf_op jit(solution)/shard_map/mjsd,jfd->mjsf/dot_general | solution.py:97
  210.9 0.0 copy-done
  211.0 7.3 %bitcast_convert_fusion = bf16[2,2048,768]{2,1,0:T(8,128)(2,1)} fusion(bf16[2,2,384,2048]{3,2,0,1:T(8,128)(2,1)S(1)} %bitcast.107, bf16[2,2,384,768]{3,2,1,0:T(8,128)(2,1)S(1)} %copy-done), kind=kOutput, calls=%fused_computation.2 | convolution fusion | flops 4834983936 | bytes 14942208 | tf_op jit(solution)/shard_map/mjsf,mjsd->jfd/dot_general | solution.py:110
  218.3 3.8 %copy.80 = bf16[2,1,2,384,768]{4,0,2,1,3:T(2,128)(2,1)} copy(bf16[2,1,2,384,768]{4,3,0,2,1:T(8,128)(2,1)S(1)} %convert_bitcast_fusion) | data formatting | bytes 4718592 | tf_op jit(solution)/shard_map/reshape | solution.py:101
  222.1 4.8 %all-to-all-start.1 = ((bf16[2,1,2,384,768]{4,0,2,1,3:T(2,128)(2,1)}), bf16[2,1,2,384,768]{4,0,2,1,3:T(2,128)(2,1)S(1)}, u32[]{:S(2)}, u32[]{:S(2)}) async-start(bf16[2,1,2,384,768]{4,0,2,1,3:T(2,128)(2,1)} %copy.80), calls=%async_computation.1 | async-start | bytes 4718592 | tf_op jit(solution)/shard_map/all_to_all | solution.py:100
  226.8 0.0 copy-start.3
  226.8 9.5 %multiply_reduce_fusion = (f32[2]{0:T(128)S(1)}, f32[2,768,768]{2,1,0:T(8,128)S(1)}) fusion(bf16[2,2048,768]{2,1,0:T(8,128)(2,1)} %bitcast_convert_fusion), kind=kOutput, calls=%fused_computation.10 | convolution fusion | flops 4834197504 | bytes 11010056 | tf_op jit(solution)/shard_map/efd,egd->efg/dot_general | solution.py:49
  236.3 0.0 copy-start.4
  236.4 2.2 copy-done.4
  238.5 0.0 copy-done.3
  238.5 3.8 %add_convert_fusion.1 = bf16[2,768,768]{2,1,0:T(8,128)(2,1)} fusion(f32[768,768]{1,0:T(8,128)S(1)} %copy-done.3, f32[2,768,768]{2,1,0:T(8,128)S(1)} %get-tuple-element.7, f32[2]{0:T(128)S(1)} %get-tuple-element.5), kind=kOutput, calls=%fused_computation.9 | convolution fusion | flops 1821376512 | bytes 9437192 | tf_op jit(solution)/shard_map/efg,egh->efh/dot_general | solution.py:56
  242.3 9.9 %fusion.7 = f32[2,768,768]{2,1,0:T(8,128)} fusion(bf16[2,768,768]{2,1,0:T(8,128)(2,1)} %add_convert_fusion.1, f32[2,768,768]{2,1,0:T(8,128)} %copy-done.4, f32[2]{0:T(128)S(1)} %get-tuple-element.5), kind=kOutput, calls=%fused_computation.20 | convolution fusion | flops 3627417600 | bytes 11796488 | tf_op jit(solution)/shard_map/efg,egh->efh/dot_general | solution.py:65
  252.2 13.0 %fusion.2 = f32[2,768,768]{2,1,0:T(8,128)} fusion(bf16[2,768,768]{2,1,0:T(8,128)(2,1)} %add_convert_fusion.1, f32[2,768,768]{2,1,0:T(8,128)} %fusion.7, f32[768,768]{1,0:T(8,128)} %fusion.12), kind=kOutput, calls=%fused_computation.15 | convolution fusion | flops 3630956544 | bytes 14155776 | tf_op jit(solution)/shard_map/efg,egh->efh/dot_general | solution.py:73
  265.2 10.3 %convolution_convert_fusion = bf16[2,768,2048]{2,1,0:T(8,128)(2,1)} fusion(bf16[2,2048,768]{2,1,0:T(8,128)(2,1)} %bitcast_convert_fusion, f32[2,768,768]{2,1,0:T(8,128)} %fusion.2, f32[2]{0:T(128)S(1)} %get-tuple-element.4), kind=kOutput, calls=%fused_computation.11 | convolution fusion | flops 4837343232 | bytes 17301512 | tf_op jit(solution)/shard_map/efg,egd->efd/dot_general | solution.py:76
  275.5 4.4 %all-to-all-done.1 = bf16[2,1,2,384,768]{4,0,2,1,3:T(2,128)(2,1)S(1)} async-done(((bf16[2,1,2,384,768]{4,0,2,1,3:T(2,128)(2,1)}), bf16[2,1,2,384,768]{4,0,2,1,3:T(2,128)(2,1)S(1)}, u32[]{:S(2)}, u32[]{:S(2)}) %all-to-all-start.1) | async-done | bytes 2359328 | tf_op jit(solution)/shard_map/all_to_all | solution.py:100
  279.9 1.7 copy.81
  281.6 0.0 copy-start.1
  281.6 19.4 %gather_fusion.1 = bf16[1024,768]{1,0:T(8,128)(2,1)} fusion(bf16[2,768,768]{2,1,0:T(8,128)(2,1)} %bitcast.102, s32[1024]{0:T(1024)S(1)} %bitcast.103), kind=kCustom, calls=%fused_computation.1 | custom fusion | bytes 3153920 | tf_op jit(solution)/shard_map/vmap(jit(_take))/gather | solution.py:22
  301.1 2.8 broadcast_select_fusion
  303.8 0.0 copy-done.1
  (10 shorter events, 0.2 us)
Async XLA Ops:
  0.6 210.3 %copy-start = (bf16[2,2,384,768]{3,2,1,0:T(8,128)(2,1)S(1)}, bf16[2,2,384,768]{3,2,1,0:T(8,128)(2,1)}, u32[]{:S(2)}) copy-start(bf16[2,2,384,768]{3,2,1,0:T(8,128)(2,1)} %param.8) | copy-start | bytes 7077892
  0.6 5.0 %copy-start.2 = (bf16[2,64,2048]{2,1,0:T(8,128)(2,1)S(1)}, bf16[2,64,2048]{2,1,0:T(8,128)(2,1)}, u32[]{:S(2)}) copy-start(bf16[2,64,2048]{2,1,0:T(8,128)(2,1)} %param.7) | copy-start | bytes 1572868
  55.5 143.9 %all-to-all-start = ((bf16[16,2,1,2,24,2048]{5,4,1,3,2,0:T(8,128)(2,1)}), bf16[16,2,1,2,24,2048]{5,4,1,3,2,0:T(8,128)(2,1)}, u32[]{:S(2)}, u32[]{:S(2)}) async-start(bf16[16,2,1,2,24,2048]{5,4,1,3,2,0:T(8,128)(2,1)} %fusion.26), calls=%async_computation | async-start | bytes 12582912 | tf_op jit(solution)/shard_map/all_to_all | solution.py:14
  222.1 57.8 %all-to-all-start.1 = ((bf16[2,1,2,384,768]{4,0,2,1,3:T(2,128)(2,1)}), bf16[2,1,2,384,768]{4,0,2,1,3:T(2,128)(2,1)S(1)}, u32[]{:S(2)}, u32[]{:S(2)}) async-start(bf16[2,1,2,384,768]{4,0,2,1,3:T(2,128)(2,1)} %copy.80), calls=%async_computation.1 | async-start | bytes 4718592 | tf_op jit(solution)/shard_map/all_to_all | solution.py:100
  226.8 11.7 %copy-start.3 = (f32[768,768]{1,0:T(8,128)S(1)}, f32[768,768]{1,0:T(8,128)}, u32[]{:S(2)}) copy-start(f32[768,768]{1,0:T(8,128)} %fusion.12) | copy-start | bytes 7077892
  236.3 2.2 copy-start.4
  281.6 22.2 %copy-start.1 = (bf16[2,2,384,768]{3,2,1,0:T(8,128)(2,1)S(1)}, bf16[2,2,384,768]{3,2,1,0:T(8,128)(2,1)}, u32[]{:S(2)}) copy-start(bf16[2,2,384,768]{3,2,1,0:T(8,128)(2,1)} %param.8) | copy-start | bytes 7077892
